TPU v7x, 256 devices: a whole 4x4x8 slice. The times are simulated.
256 devices in a mesh: dp: 32 (over z, x_lo, core), tp: 8 (over x_hi, y).
Axes of the slice: x: 4 (x_hi: 2, x_lo: 2; x = x_hi * 2 + x_lo), y: 4, z: 8, core: 2. Of those that a mesh axis runs over, the one named last changes fastest.
Arguments:
- queries: bfloat16 [256, 8192], P('dp', 'tp'), may hold values from -5 to 5
- prefix_kv: bfloat16 [2, 65536, 1024], P(None, 'dp', 'tp'), may hold values from -5 to 5
- cache_kv: bfloat16 [2, 2048, 64, 1024], P(None, 'dp', None, 'tp'), may hold values from -5 to 5
- lengths: int32 [256], P('dp'), may hold values from 1 to 512, as said below
- page_table: int32 [32, 64], P('dp'), may hold values from 0 to 63, each once within a row
- owner: int32 [32], replicated, may hold values from 0 to 31, as said below
- readers: int32 [16], replicated, may hold values from 0 to 31, as said below
- w_out: bfloat16 [8192, 4096], P('tp'), may hold values from -0.5 to 0.5
Outputs:
- projected: bfloat16 [256, 4096], P('dp', 'tp')
Inputs may be any that keep to these rules, and one draw needn't show every extreme that they name: `lengths`: at most 512, reached by some request in every draw. `page_table`: each row holds every page id of its replica once. `owner`: every replica index once. `readers`: 16 distinct replica indices, none of them owner[0].
All inputs are finite; a program needn't handle non-finite values.
Results may differ from a plain program's by a relative error of at most 0.0051.
Values may be sent and summed in bfloat16 or wider, within the bound.
A program may use at most 64 MiB of HBM per device.

v0:
```python
import jax
import jax.numpy as jnp
from jax import lax
from jax.sharding import PartitionSpec as P

HD = 128
PREFIX = 2048
PAGE = 64


def padded_to(lines, length):
    spare = -lines.shape[0] % length
    if not spare:
        return lines
    return jnp.concatenate([lines, jnp.zeros((spare, *lines.shape[1:]), lines.dtype)])


def broadcast_by_parts(value, axis, root):
    lines = jnp.where(lax.axis_index(axis) == root, value, jnp.zeros_like(value)).reshape(
        -1, *value.shape[1:][-1:]
    )
    padded = padded_to(lines, lax.axis_size(axis))
    own = lax.psum_scatter(padded, axis, scatter_dimension=0, tiled=True)
    return lax.all_gather(own, axis, axis=0, tiled=True)[: len(lines)].reshape(value.shape)


def cut_along(value, dim, length):
    lengths = value.shape
    tiles = value.reshape(*lengths[:dim], length, lengths[dim] // length, *lengths[dim + 1 :])
    return jnp.moveaxis(tiles, dim, 0)


def sum_at_owner(value, axis, dim):
    length = lax.axis_size(axis)
    tiles = lax.all_to_all(cut_along(value, dim, length), axis, 0, 0, tiled=True)
    return jnp.sum(tiles, axis=0)


def shards(queries, prefix_kv, cache_kv, lengths, page_table, owner, readers, w_out):
    rows = queries.shape[0]
    heads_here = queries.shape[1] // HD
    groups_here = prefix_kv.shape[2] // HD
    group = heads_here // groups_here
    maxpages = page_table.shape[1] // rows
    scale = 1.0 / HD**0.5
    replica_id = lax.axis_index("dp")
    matches = readers == replica_id
    is_reader = jnp.any(matches)
    query = queries.reshape(rows, groups_here, group, HD)
    pages = page_table[0].reshape(rows, maxpages)
    resident = cache_kv[:, pages].reshape(2, rows, maxpages * PAGE, groups_here, HD)
    s_res = (
        jnp.einsum("bkgd,btkd->bkgt", query, resident[0], preferred_element_type=jnp.float32)
        * scale
    )
    inside = jnp.arange(maxpages * PAGE, dtype=jnp.int32)[None, :] < lengths[:, None]
    s_res = jnp.where(inside[:, None, None, :], s_res, -jnp.inf)
    top_res = jnp.max(s_res, axis=-1)
    shared = broadcast_by_parts(prefix_kv, "dp", owner[0])
    shared = shared.reshape(2, PREFIX, groups_here, HD)
    s_pre = (
        jnp.einsum("bkgd,tkd->bkgt", query, shared[0], preferred_element_type=jnp.float32) * scale
    )
    s_pre = jnp.where(is_reader, s_pre, -jnp.inf)
    top = jnp.maximum(top_res, jnp.max(s_pre, axis=-1))
    e_pre = jnp.exp(s_pre - top[..., None])
    den_pre = jnp.sum(e_pre, axis=-1)
    num_pre = jnp.einsum(
        "bkgt,tkd->bkgd", e_pre.astype(jnp.bfloat16), shared[1], preferred_element_type=jnp.float32
    )
    e_res = jnp.exp(s_res - top[..., None])
    den = jnp.sum(e_res, axis=-1) + den_pre
    num = (
        jnp.einsum(
            "bkgt,btkd->bkgd",
            e_res.astype(jnp.bfloat16),
            resident[1],
            preferred_element_type=jnp.float32,
        )
        + num_pre
    )
    attn = (num / den[..., None]).astype(jnp.bfloat16).reshape(rows, heads_here * HD)
    partial_out = jnp.dot(attn, w_out, preferred_element_type=jnp.float32)
    return sum_at_owner(partial_out, "tp", 1).astype(jnp.bfloat16)


def solution(mesh):
    placed = (
        P("dp", "tp"),
        P(None, "dp", "tp"),
        P(None, "dp", None, "tp"),
        P("dp"),
        P("dp", None),
        P(),
        P(),
        P("tp", None),
    )
    return jax.shard_map(
        shards, mesh=mesh, in_specs=placed, out_specs=P("dp", "tp"), check_vma=False
    )
```

profile of v0, /device:TPU:1, one launch (start us, length us, event | category | flops | bytes accessed | tf_op | source)
XLA Modules:
  0.0 223.7 jit_solution(934141285971091137)
XLA Ops:
  6.5 0.0 copy-start
  6.5 0.0 copy-start.4
  6.5 0.0 reduce-scatter.2.cloned.1.call-start
  7.4 1.1 broadcast_select_fusion
  8.4 0.0 reduce-scatter.2.cloned.1.call-update
  8.5 0.0 all-gather.2.cloned.1.call-start
  8.5 118.1 %reduce-scatter.2.cloned.1.call-done = bf16[128,128]{1,0:T(8,128)(2,1)} async-done(((bf16[4096,128]{1,0:T(8,128)(2,1)}), bf16[128,128]{1,0:T(8,128)(2,1)}) %reduce-scatter.2.cloned.1.call-update) | async-done | bytes 32784 | tf_op jit(solution)/shard_map/reduce_scatter | solution.py:23
  126.6 0.0 all-gather.2.cloned.1.call-update
  126.6 0.5 broadcast.55
  127.1 0.0 copy-done.4
  127.1 0.7 reduce.9
  127.8 0.1 reshape_squeeze.3
  127.9 0.1 reshape.140
  128.0 0.0 copy-done
  128.0 2.2 gather_fusion
  130.2 3.2 %copy.23 = bf16[8,8,2,64,128]{4,3,1,0,2:T(8,128)(2,1)} copy(bf16[8,8,2,64,128]{4,3,2,1,0:T(8,128)(2,1)} %bitcast.54) | data formatting | bytes 4194304 | tf_op jit(solution)/shard_map/gather | solution.py:51
  133.4 0.0 copy-start.5
  133.4 0.0 copy-start.2
  133.4 12.0 %copy.13 = bf16[4096,1024]{1,0:T(8,128)(2,1)} copy(bf16[4096,1024]{0,1:T(8,128)(2,1)} %bitcast.55) | data formatting | bytes 16777216 | tf_op jit(solution)/shard_map/dot_general | solution.py:83
  145.4 0.0 copy-done.5
  145.4 0.6 compare_reduce_fusion
  146.0 0.0 copy-done.2
  146.0 0.1 iota_compare_fusion
  146.1 0.0 copy-start.1
  146.1 1.8 fusion.18
  147.9 0.0 copy-done.1
  147.9 0.5 fusion.19
  148.4 46.1 %all-gather.2.cloned.1.call-done = bf16[4096,128]{1,0:T(8,128)(2,1)} async-done(((bf16[128,128]{1,0:T(8,128)(2,1)}), bf16[4096,128]{1,0:T(8,128)(2,1)}) %all-gather.2.cloned.1.call-update) | async-done | bytes 1048592 | tf_op jit(solution)/shard_map/all_gather | solution.py:24
  194.5 0.0 copy-start.3
  194.5 2.1 fusion.20
  196.7 0.2 fusion.12
  196.8 0.3 convolution_bitcast_fusion.2
  197.1 0.2 fusion.7
  197.4 0.0 copy-done.3
  197.4 0.3 fusion.6
  197.7 5.6 %convolution_bitcast_fusion = f32[8,8,512]{2,1,0:T(8,128)S(1)} fusion(bf16[8,1024,1]{1,0,2:T(8,128)(2,1)S(1)} %reshape.149, bf16[8,512,1024]{2,1,0:T(8,128)(2,1)} %bitcast.53), kind=kOutput, calls=%fused_computation.5 | convolution fusion | flops 67108864 | bytes 8536064 | tf_op jit(solution)/shard_map/dot_general | solution.py:83
  203.3 12.9 %all_to_all.5 = f32[8,8,512]{2,1,0:T(8,128)S(1)} all-to-all(f32[8,8,512]{2,1,0:T(8,128)S(1)} %convolution_bitcast_fusion), channel_id=1, replica_groups=mesh['dp'=32,'tp'=8] {'tp'}, dimensions={0} | all-to-all | bytes 262144 | tf_op jit(solution)/shard_map/all_to_all | solution.py:35
  216.2 0.6 reduce_sum.29
  (5 shorter events, 0.0 us)
Async XLA Ops:
  6.5 121.5 %copy-start = (bf16[2,64,64,128]{3,2,1,0:T(8,128)(2,1)S(1)}, bf16[2,64,64,128]{3,2,1,0:T(8,128)(2,1)}, u32[]{:S(2)}) copy-start(bf16[2,64,64,128]{3,2,1,0:T(8,128)(2,1)} %param.10) | copy-start | bytes 6291460
  6.5 120.6 %copy-start.4 = (s32[1,64]{1,0:T(1,128)S(1)}, s32[1,64]{1,0:T(1,128)}, u32[]{:S(2)}) copy-start(s32[1,64]{1,0:T(1,128)} %param.12) | copy-start | bytes 772
  6.5 120.1 %reduce-scatter.2.cloned.1.call-start = ((), (), s32[]{:S(2)}) async-start(), calls=%async_computation.2 | async-start | bytes 1081344 | tf_op jit(solution)/shard_map/reduce_scatter | solution.py:23
  8.5 186.0 %all-gather.2.cloned.1.call-start = ((), (), s32[]{:S(2)}) async-start(), calls=%async_computation.3 | async-start | bytes 1081344 | tf_op jit(solution)/shard_map/all_gather | solution.py:24
  133.4 12.0 %copy-start.5 = (s32[16]{0:T(128)S(1)}, s32[16]{0:T(128)}, u32[]{:S(2)}) copy-start(s32[16]{0:T(128)} %param.14) | copy-start | bytes 196
  133.4 12.7 %copy-start.2 = (s32[8]{0:T(128)S(1)}, s32[8]{0:T(128)}, u32[]{:S(2)}) copy-start(s32[8]{0:T(128)} %param.11) | copy-start | bytes 100
  146.1 1.8 copy-start.1
  194.5 2.9 %copy-start.3 = (bf16[4096,128]{1,0:T(8,128)(2,1)S(1)}, bf16[4096,128]{1,0:T(8,128)(2,1)}, u32[]{:S(2)}) copy-start(bf16[4096,128]{1,0:T(8,128)(2,1)} %all-gather.2.cloned.1.call-done) | copy-start | bytes 3145732
Sparse Core Ops, SparseCore 0:
  9.9 116.7 reduce-scatter.1
  128.6 65.8 all-gather.1
where the time goes:
time: 224 us
  waiting for transfers between devices  164 us (73%)
  local copies, waits for them, and re-layouts  19.9 us (9%)
  between operations  14.3 us (6%)
  blocking collectives  12.9 us (6%)
  matrix products  8.83 us (4%)
  other arithmetic  3.49 us (2%)
    reduce_scatter x1, waiting for transfers between devices, broadcast_by_parts(): own = lax.psum_scatter(padded, axis, scatter_dimension=0, tiled=True)  118 us
    all_gather x1, waiting for transfers between devices, broadcast_by_parts(): lax.all_gather(own, axis, axis=0, tiled=True)[:len(lines)]  46.1 us
    all_to_all x1, blocking collectives, sum_at_owner(): lax.all_to_all(cut_along(value, dim, length), axis, 0, 0, tiled=True)  12.9 us
    dot_general x1, local copies, waits for them, and re-layouts, shards(): partial_out = jnp.dot(attn, w_out, preferred_element_type=jnp.float32)  12 us
    dot_general x1, matrix products, shards(): partial_out = jnp.dot(attn, w_out, preferred_element_type=jnp.float32)  5.64 us
    gather x2, local copies, waits for them, and re-layouts, shards(): cache_kv[:, pages].reshape(2, rows, maxpages * PAGE, groups_here, HD)  5.39 us
  transfers between devices with their start and end apart: 2, of which 2 were waited for; matrix products, arithmetic and copies ran while one was open for 10% of the time, Pallas kernels for 0%

commit v1 on v0

--- a/solution.py
+++ b/solution.py
@@ -21,7 +21,12 @@
     )
     padded = padded_to(lines, lax.axis_size(axis))
     own = lax.psum_scatter(padded, axis, scatter_dimension=0, tiled=True)
-    return lax.all_gather(own, axis, axis=0, tiled=True)[: len(lines)].reshape(value.shape)
+    return jnp.concatenate(
+        jax.lax.all_to_all(
+            jnp.stack([own for _ in range(jax.lax.psum(1, axis))], axis=0), axis, 0, 0
+        ),
+        axis=0,
+    )[: len(lines)].reshape(value.shape)
 
 
 def cut_along(value, dim, length):

time: 224 us -> 195 us (0.87)
  waiting for transfers between devices: 164 us -> 124 us
  starting transfers between devices: 0.04 us -> 8.78 us
  local copies, waits for them, and re-layouts: 19.9 us -> 22.8 us
    all_gather x1 -> x0, waiting for transfers between devices: 46.1 us -> none  [broadcast_by_parts(): lax.all_gather(own, axis, axis=0, tiled=True)[:len(lines)]]
    all_to_all x0 -> x1, starting transfers between devices: none -> 8.78 us  [broadcast_by_parts(): jax.lax.all_to_all(jnp.stack([own for _ in range(jax.lax.psum(1, axis))],...]
    all_to_all x0 -> x1, waiting for transfers between devices: none -> 5.53 us  [broadcast_by_parts(): jax.lax.all_to_all(jnp.stack([own for _ in range(jax.lax.psum(1, axis))],...]
  transfers between devices with their start and end apart: 2 -> 2, of which waited for: 2 -> 2; matrix products, arithmetic and copies ran while one was open for 10% -> 12% of each run, Pallas kernels for 0% -> 0%
where the time goes in v1:
time: 195 us; the launch traced here: 194 us
  waiting for transfers between devices  124 us (64%)
  local copies, waits for them, and re-layouts  22.8 us (12%)
  between operations  14.3 us (7%)
  blocking collectives  13.1 us (7%)
  starting transfers between devices  8.78 us (5%)
  matrix products  7.78 us (4%)
  other arithmetic  3.49 us (2%)
    reduce_scatter x1, waiting for transfers between devices, broadcast_by_parts(): own = lax.psum_scatter(padded, axis, scatter_dimension=0, tiled=True)  118 us
    all_to_all x1, blocking collectives, sum_at_owner(): lax.all_to_all(cut_along(value, dim, length), axis, 0, 0, tiled=True)  13.1 us
    dot_general x1, local copies, waits for them, and re-layouts, shards(): partial_out = jnp.dot(attn, w_out, preferred_element_type=jnp.float32)  12 us
    all_to_all x1, starting transfers between devices, broadcast_by_parts(): jax.lax.all_to_all(jnp.stack([own for _ in range(jax.lax.psum(1, axis))],...  8.78 us
    dot_general x1, matrix products, shards(): partial_out = jnp.dot(attn, w_out, preferred_element_type=jnp.float32)  5.64 us
    all_to_all x1, waiting for transfers between devices, broadcast_by_parts(): jax.lax.all_to_all(jnp.stack([own for _ in range(jax.lax.psum(1, axis))],...  5.53 us
    gather x2, local copies, waits for them, and re-layouts, shards(): cache_kv[:, pages].reshape(2, rows, maxpages * PAGE, groups_here, HD)  5.39 us
  transfers between devices with their start and end apart: 2, of which 2 were waited for; matrix products, arithmetic and copies ran while one was open for 12% of the time, Pallas kernels for 0%

profile of v1, /device:TPU:1, one launch (start us, length us, event | category | flops | bytes accessed | tf_op | source)
XLA Modules:
  0.0 193.9 jit_solution(17274023574642356115)
XLA Ops:
  6.5 0.0 copy-start
  6.5 0.0 reduce-scatter.2.cloned.1.call-start
  7.3 1.1 broadcast_select_fusion
  8.4 0.0 copy-start.4
  8.4 0.0 reduce-scatter.2.cloned.1.call-update
  8.4 118.2 %reduce-scatter.2.cloned.1.call-done = bf16[128,128]{1,0:T(8,128)(2,1)} async-done(((bf16[4096,128]{1,0:T(8,128)(2,1)}), bf16[128,128]{1,0:T(8,128)(2,1)}) %reduce-scatter.2.cloned.1.call-update) | async-done | bytes 32784 | tf_op jit(solution)/shard_map/reduce_scatter | solution.py:23
  126.6 2.0 %stack.2 = bf16[32,128,128]{2,1,0:T(8,128)(2,1)} broadcast(bf16[128,128]{1,0:T(8,128)(2,1)} %reduce-scatter.2.cloned.1.call-done), dimensions={1,2} | broadcast | bytes 1081344 | tf_op jit(solution)/shard_map/stack | solution.py:26
  128.6 8.8 %all-to-all-start = ((bf16[32,128,128]{2,1,0:T(8,128)(2,1)}), bf16[32,128,128]{2,1,0:T(8,128)(2,1)S(1)}, u32[]{:S(2)}, u32[]{:S(2)}) async-start(bf16[32,128,128]{2,1,0:T(8,128)(2,1)} %stack.2), calls=%async_computation.1 | async-start | bytes 2097152 | tf_op jit(solution)/shard_map/all_to_all | solution.py:25
  137.4 0.5 broadcast.57
  137.9 0.0 copy-done.4
  137.9 0.7 reduce.9
  138.5 0.1 reshape_squeeze.3
  138.6 0.1 reshape.148
  138.7 0.0 copy-done
  138.7 2.2 %gather_fusion = bf16[64,2,64,128]{3,2,1,0:T(8,128)(2,1)} fusion(bf16[2,64,64,128]{3,2,1,0:T(8,128)(2,1)S(1)} %copy-done, s32[1024]{0:T(1024)S(1)} %pad_clamp_fusion), kind=kCustom, calls=%fused_computation | custom fusion | bytes 4194560 | tf_op jit(solution)/shard_map/gather | solution.py:56
  140.9 3.2 %copy.23 = bf16[8,8,2,64,128]{4,3,1,0,2:T(8,128)(2,1)} copy(bf16[8,8,2,64,128]{4,3,2,1,0:T(8,128)(2,1)} %bitcast.54) | data formatting | bytes 4194304 | tf_op jit(solution)/shard_map/gather | solution.py:56
  144.1 0.0 copy-start.5
  144.1 0.0 copy-start.3
  144.1 12.0 %copy.13 = bf16[4096,1024]{1,0:T(8,128)(2,1)} copy(bf16[4096,1024]{0,1:T(8,128)(2,1)} %bitcast.55) | data formatting | bytes 16777216 | tf_op jit(solution)/shard_map/dot_general | solution.py:88
  156.1 0.0 copy-done.5
  156.1 0.6 compare_reduce_fusion
  156.7 0.0 copy-done.3
  156.7 0.1 iota_compare_fusion
  156.8 0.0 copy-start.2
  156.8 2.7 %fusion.18 = (bf16[1,8,8,64,128]{4,3,2,1,0:T(8,128)(2,1)S(1)}, bf16[1,8,8,64,128]{4,3,2,1,0:T(8,128)(2,1)}) fusion(bf16[2,8,8,64,128]{4,3,2,1,0:T(8,128)(2,1)} %bitcast.56), kind=kLoop, calls=%fused_computation.30 | loop fusion | bytes 4194304 | tf_op jit(solution)/shard_map/slice | solution.py:58
  159.5 0.0 copy-done.2
  159.5 0.5 fusion.20
  160.0 5.5 %all-to-all-done = bf16[32,128,128]{2,1,0:T(8,128)(2,1)S(1)} async-done(((bf16[32,128,128]{2,1,0:T(8,128)(2,1)}), bf16[32,128,128]{2,1,0:T(8,128)(2,1)S(1)}, u32[]{:S(2)}, u32[]{:S(2)}) %all-to-all-start) | async-done | bytes 1048608 | tf_op jit(solution)/shard_map/all_to_all | solution.py:25
  165.5 0.0 copy-start.1
  165.5 0.1 fusion.19
  165.6 1.1 fusion.21
  166.7 0.2 fusion.12
  166.9 0.0 copy-done.1
  166.9 0.3 convolution_bitcast_fusion.2
  167.2 0.2 fusion.7
  167.4 0.3 fusion.6
  167.8 5.6 %convolution_bitcast_fusion = f32[8,8,512]{2,1,0:T(8,128)S(1)} fusion(bf16[8,1024,1]{1,0,2:T(8,128)(2,1)S(1)} %reshape.157, bf16[8,512,1024]{2,1,0:T(8,128)(2,1)} %bitcast.53), kind=kOutput, calls=%fused_computation.5 | convolution fusion | flops 67108864 | bytes 8536064 | tf_op jit(solution)/shard_map/dot_general | solution.py:88
  173.4 13.1 %all_to_all.10 = f32[8,8,512]{2,1,0:T(8,128)S(1)} all-to-all(f32[8,8,512]{2,1,0:T(8,128)S(1)} %convolution_bitcast_fusion), channel_id=1, replica_groups=mesh['dp'=32,'tp'=8] {'tp'}, dimensions={0} | all-to-all | bytes 262144 | tf_op jit(solution)/shard_map/all_to_all | solution.py:40
  186.5 0.6 reduce_sum.29
  (5 shorter events, 0.0 us)
Async XLA Ops:
  6.5 132.2 %copy-start = (bf16[2,64,64,128]{3,2,1,0:T(8,128)(2,1)S(1)}, bf16[2,64,64,128]{3,2,1,0:T(8,128)(2,1)}, u32[]{:S(2)}) copy-start(bf16[2,64,64,128]{3,2,1,0:T(8,128)(2,1)} %param.10) | copy-start | bytes 6291460
  6.5 120.1 %reduce-scatter.2.cloned.1.call-start = ((), (), s32[]{:S(2)}) async-start(), calls=%async_computation.3 | async-start | bytes 1081344 | tf_op jit(solution)/shard_map/reduce_scatter | solution.py:23
  8.4 129.5 %copy-start.4 = (s32[1,64]{1,0:T(1,128)S(1)}, s32[1,64]{1,0:T(1,128)}, u32[]{:S(2)}) copy-start(s32[1,64]{1,0:T(1,128)} %param.12) | copy-start | bytes 772
  128.6 36.9 %all-to-all-start = ((bf16[32,128,128]{2,1,0:T(8,128)(2,1)}), bf16[32,128,128]{2,1,0:T(8,128)(2,1)S(1)}, u32[]{:S(2)}, u32[]{:S(2)}) async-start(bf16[32,128,128]{2,1,0:T(8,128)(2,1)} %stack.2), calls=%async_computation.1 | async-start | bytes 2097152 | tf_op jit(solution)/shard_map/all_to_all | solution.py:25
  144.1 12.0 %copy-start.5 = (s32[16]{0:T(128)S(1)}, s32[16]{0:T(128)}, u32[]{:S(2)}) copy-start(s32[16]{0:T(128)} %param.14) | copy-start | bytes 196
  144.1 12.6 %copy-start.3 = (s32[8]{0:T(128)S(1)}, s32[8]{0:T(128)}, u32[]{:S(2)}) copy-start(s32[8]{0:T(128)} %param.11) | copy-start | bytes 100
  156.8 2.7 %copy-start.2 = (bf16[8,1024]{1,0:T(8,128)(2,1)S(1)}, bf16[8,1024]{1,0:T(8,128)(2,1)}, u32[]{:S(2)}) copy-start(bf16[8,1024]{1,0:T(8,128)(2,1)} %param.8) | copy-start | bytes 49156
  165.5 1.4 copy-start.1
Sparse Core Ops, SparseCore 0:
  9.9 116.7 reduce-scatter.1
